TPU v7x, 32 devices: a whole 2x2x4 slice. The times are simulated.
32 devices in a mesh: pair: 8 (over z, x), rows: 4 (over y, core).
Axes of the slice: x: 2, y: 2, z: 4, core: 2. Of those that a mesh axis runs over, the one named last changes fastest.
Arguments:
- matrix: float32 [16384, 2048], P('rows', 'pair')
- plan: int32 [3, 8], P(None, 'pair'), may hold values 0 or 1
Outputs:
- rotated: float32 [16384, 2048], P('rows', 'pair')
- offness: float32 [3], replicated
All inputs are finite; a program needn't handle non-finite values. No bound on the sum of `plan` on one device may be relied on, other than what follows from the above.
Results may differ from a plain program's by a relative error of at most 0.00025.
Values sent between devices are 32-bit elements; how exact they have to be, the bound alone decides.
A program may use at most 64 MiB of HBM per device.

v0:
```python
import jax
import jax.numpy as jnp
from jax import lax
from jax.sharding import PartitionSpec as P

ROUNDS = 3


def from_behind(x, axis, by):
    peers = lax.axis_size(axis)
    return lax.ppermute(x, axis, [(i, (i + by) % peers) for i in range(peers)])


def off_total(value):
    return lax.psum(value, "pair")


def pass_on(block):
    return from_behind(block, "pair", 1)


def make_rotation(gram, mean_sq, eye, weights):
    diagonal = jnp.diagonal(gram)
    denom = diagonal[:, None] + diagonal[None, :] + mean_sq
    skew = gram * (weights[None, :] - weights[:, None]) / denom
    square = jnp.dot(skew, skew, precision=lax.Precision.HIGHEST)
    plus = eye + skew
    numer = jnp.dot(plus, plus, precision=lax.Precision.HIGHEST)
    lower = jnp.linalg.cholesky(eye - square)
    return jax.scipy.linalg.cho_solve((lower, True), numer)


def local(matrix, plan):
    width = matrix.shape[1]
    half = width // 2
    pair_count = lax.axis_size("pair")
    ncols_all = width * pair_count
    eye = jnp.eye(width, dtype=jnp.float32)
    weights = jnp.arange(width, dtype=jnp.float32) / jnp.float32(width - 1)
    mean_sq = lax.psum(jnp.sum(matrix * matrix), ("pair", "rows")) / ncols_all
    current = matrix
    values = []
    for step in range(ROUNDS):
        partial_gram = lax.dot_general(
            current,
            current,
            (((0,), (0,)), ((), ())),
            precision=lax.Precision.HIGHEST,
            preferred_element_type=jnp.float32,
        )
        gram = lax.psum(partial_gram, "rows")
        offdiag = gram * (1.0 - eye)
        off_local = jnp.sum(offdiag * offdiag)
        if step == 0:
            total_off = off_total(off_local)
        else:
            total_off = off_total(off_local)
        values.append(jnp.sqrt(total_off / (pair_count * width * (width - 1))) / mean_sq)
        rotation = make_rotation(gram, mean_sq, eye, weights)
        keep_last = plan[step, 0] == 1
        turned = jnp.dot(current, rotation, precision=lax.Precision.HIGHEST)
        first_half = turned[:, :half]
        second_half = turned[:, half:]
        kept = jnp.where(keep_last, second_half, first_half)
        moving = jnp.where(keep_last, first_half, second_half)
        arrived = pass_on(moving)
        current = jnp.concatenate([kept, arrived], axis=1)
    return (current, jnp.stack(values))


def solution(mesh):
    in_specs = (P("rows", "pair"), P(None, "pair"))
    out_specs = (P("rows", "pair"), P())
    return jax.shard_map(local, mesh=mesh, in_specs=in_specs, out_specs=out_specs, check_vma=False)
```

profile of v0, /device:TPU:0, one launch (start us, length us, event | category | flops | bytes accessed | tf_op | source)
XLA Modules:
  0.0 539.2 jit_solution(11518162019927558470)
XLA Ops:
  7.2 10.9 %fusion.76 = f32[256,256]{0,1:T(8,128)} fusion(f32[4096,256]{1,0:T(8,128)} %param.5), kind=kOutput, calls=%fused_computation.150 | convolution fusion | flops 3221225472 | bytes 4456448 | tf_op jit(solution)/shard_map/dot_general | solution.py:44
  18.2 3.9 multiply_reduce_fusion
  22.1 0.7 fusion.75
  22.7 42.5 %psum.50 = f32[]{:T(128)} all-reduce(f32[]{:T(128)} %multiply_reduce_fusion), channel_id=1, replica_groups=mesh['pair'=8,'rows'=4] {'pair','rows'}, use_global_device_ids=true, to_apply=%region_2.0 | all-reduce | flops 1 | bytes 8 | tf_op jit(solution)/shard_map/psum | solution.py:40
  66.6 2.7 gather_fusion
  69.2 1.6 convolution_subtract_fusion.2
  71.0 11.7 %cholesky.172 = f32[128,128]{1,0:T(8,128)S(1)} custom-call(f32[128,128]{1,0:T(8,128)S(1)} %cholesky.270), custom_call_target="Cholesky" | custom-call | tf_op jit(solution)/shard_map/jit(cholesky)/cholesky | solution.py:29
  82.8 9.8 %custom-call.23 = f32[1,128,128]{1,2,0:T(8,128)S(1)} custom-call(f32[1,128,128]{2,1,0:T(8,128)S(1)} %get-tuple-element.81), custom_call_target="InvertDiagBlocksLowerTriangular" | custom-call | tf_op jit(solution)/shard_map/jit(cholesky)/cholesky | solution.py:29
  93.1 11.7 %cholesky.189 = f32[128,128]{1,0:T(8,128)S(1)} custom-call(f32[128,128]{1,0:T(8,128)S(1)} %convolution_subtract_fusion.11), custom_call_target="Cholesky" | custom-call | tf_op jit(solution)/shard_map/jit(cholesky)/cholesky | solution.py:29
  104.8 0.6 compare_reduce_fusion.4
  106.9 4.0 while.6
  107.5 1.4 bitcast_dynamic-update-slice_fusion.6
  109.5 1.4 bitcast_dynamic-update-slice_fusion.6
  110.9 19.8 %custom-call.24 = f32[2,128,128]{1,2,0:T(8,128)S(1)} custom-call(f32[2,128,128]{2,1,0:T(8,128)S(1)} %get-tuple-element.24), custom_call_target="InvertDiagBlocksLowerTriangular" | custom-call | tf_op jit(solution)/shard_map/jit(_cho_solve)/triangular_solve | solution.py:30
  130.8 0.8 fusion.16
  133.3 8.8 %convolution_bitcast_fusion = f32[4096,256]{0,1:T(8,128)S(1)} fusion(f32[4096,256]{1,0:T(8,128)} %param.5, f32[128,256]{1,0:T(8,128)S(1)} %fusion.47, f32[128,256]{1,0:T(8,128)S(1)} %fusion.46), kind=kOutput, calls=%fused_computation.9 | convolution fusion | flops 3221291008 | bytes 8650752 | tf_op jit(solution)/shard_map/dot_general | solution.py:61
  142.5 2.3 collective-permute-start
  144.8 47.0 %collective-permute-done = f32[4096,128]{0,1:T(8,128)S(1)} collective-permute-done((f32[4096,128]{0,1:T(8,128)S(1)}, f32[4096,128]{0,1:T(8,128)S(1)}, u32[]{:S(2)}, u32[]{:S(2)}) %collective-permute-start) | collective-permute-done | bytes 2097184 | tf_op jit(solution)/shard_map/ppermute | solution.py:11
  191.8 1.3 copy-done.5
  193.1 4.2 fusion.3
  198.2 28.8 %all-reduce.8.cloned.1.call-done = f32[256,256]{0,1:T(8,128)} async-done(((f32[256,256]{0,1:T(8,128)}), f32[256,256]{0,1:T(8,128)}) %all-reduce.8.cloned.1.call-update) | async-done | bytes 262160 | tf_op jit(solution)/shard_map/psum | solution.py:51
  227.0 2.7 gather_fusion.1
  229.7 1.6 convolution_subtract_fusion.1
  231.4 11.7 %cholesky.206 = f32[128,128]{1,0:T(8,128)S(1)} custom-call(f32[128,128]{1,0:T(8,128)S(1)} %cholesky.273), custom_call_target="Cholesky" | custom-call | tf_op jit(solution)/shard_map/jit(cholesky)/cholesky | solution.py:29
  243.2 0.7 compare_reduce_fusion.3
  243.9 9.8 %custom-call.25 = f32[1,128,128]{1,2,0:T(8,128)S(1)} custom-call(f32[1,128,128]{2,1,0:T(8,128)S(1)} %get-tuple-element.77), custom_call_target="InvertDiagBlocksLowerTriangular" | custom-call | tf_op jit(solution)/shard_map/jit(cholesky)/cholesky | solution.py:29
  254.2 11.7 %cholesky.223 = f32[128,128]{1,0:T(8,128)S(1)} custom-call(f32[128,128]{1,0:T(8,128)S(1)} %convolution_subtract_fusion.10), custom_call_target="Cholesky" | custom-call | tf_op jit(solution)/shard_map/jit(cholesky)/cholesky | solution.py:29
  266.0 0.7 compare_reduce_fusion.2
  268.0 4.5 while.7
  268.4 0.7 fusion.105
  269.1 1.3 bitcast_dynamic-update-slice_fusion.7
  270.4 0.7 fusion.105
  271.1 1.3 bitcast_dynamic-update-slice_fusion.7
  272.5 19.7 %custom-call.26 = f32[2,128,128]{1,2,0:T(8,128)S(1)} custom-call(f32[2,128,128]{2,1,0:T(8,128)S(1)} %get-tuple-element.25), custom_call_target="InvertDiagBlocksLowerTriangular" | custom-call | tf_op jit(solution)/shard_map/jit(_cho_solve)/triangular_solve | solution.py:30
  292.2 0.8 fusion.17
  294.7 4.0 fusion.2
  299.0 1.7 collective-permute-start.1
  300.7 47.2 %collective-permute-done.1 = f32[4096,128]{0,1:T(8,128)S(1)} collective-permute-done((f32[4096,128]{0,1:T(8,128)S(1)}, f32[4096,128]{0,1:T(8,128)S(1)}, u32[]{:S(2)}, u32[]{:S(2)}) %collective-permute-start.1) | collective-permute-done | bytes 2097184 | tf_op jit(solution)/shard_map/ppermute | solution.py:11
  348.0 1.3 copy-done.3
  349.3 4.2 fusion.1
  354.1 29.9 %all-reduce.10.cloned.1.call-done = f32[256,256]{0,1:T(8,128)} async-done(((f32[256,256]{0,1:T(8,128)}), f32[256,256]{0,1:T(8,128)}) %all-reduce.10.cloned.1.call-update) | async-done | bytes 262160 | tf_op jit(solution)/shard_map/psum | solution.py:51
  384.0 2.7 gather_fusion.2
  386.7 1.6 convolution_subtract_fusion
  388.4 0.7 copy-done.7
  389.1 11.7 %cholesky.240 = f32[128,128]{1,0:T(8,128)S(1)} custom-call(f32[128,128]{1,0:T(8,128)S(1)} %cholesky.276), custom_call_target="Cholesky" | custom-call | tf_op jit(solution)/shard_map/jit(cholesky)/cholesky | solution.py:29
  400.9 0.6 compare_reduce_fusion.1
  401.5 9.8 %custom-call.27 = f32[1,128,128]{1,2,0:T(8,128)S(1)} custom-call(f32[1,128,128]{2,1,0:T(8,128)S(1)} %get-tuple-element.73), custom_call_target="InvertDiagBlocksLowerTriangular" | custom-call | tf_op jit(solution)/shard_map/jit(cholesky)/cholesky | solution.py:29
  411.4 1.0 constant_dynamic-update-slice_fusion
  412.4 1.1 convolution_subtract_fusion.9
  413.5 11.9 %cholesky.257 = f32[128,128]{1,0:T(8,128)S(1)} custom-call(f32[128,128]{1,0:T(8,128)S(1)} %convolution_subtract_fusion.9), custom_call_target="Cholesky" | custom-call | tf_op jit(solution)/shard_map/jit(cholesky)/cholesky | solution.py:29
  427.4 3.8 while.8
  428.0 1.3 bitcast_dynamic-update-slice_fusion.8
  429.9 1.3 bitcast_dynamic-update-slice_fusion.8
  431.2 19.7 %custom-call.28 = f32[2,128,128]{1,2,0:T(8,128)S(1)} custom-call(f32[2,128,128]{2,1,0:T(8,128)S(1)} %get-tuple-element.26), custom_call_target="InvertDiagBlocksLowerTriangular" | custom-call | tf_op jit(solution)/shard_map/jit(_cho_solve)/triangular_solve | solution.py:30
  450.9 0.8 fusion.18
  453.5 4.0 fusion
  457.5 1.7 slice_select_fusion.1
  459.2 1.5 collective-permute-start.2
  460.6 0.8 fusion.8
  461.4 0.7 fusion.10
  462.0 0.7 fusion.12
  462.7 57.4 %all-reduce.1 = (f32[]{:T(128)}, f32[]{:T(128)}, f32[]{:T(128)}) all-reduce(f32[]{:T(128)} %fusion.12, f32[]{:T(128)} %fusion.10, f32[]{:T(128)} %fusion.8), channel_id=1, replica_groups=mesh['pair'=8,'rows'=4] {'pair'}, use_global_device_ids=true, to_apply=%region_14.17 | all-reduce | flops 3 | bytes 24 | tf_op jit(solution)/shard_map/psum | solution.py:15
  522.9 3.9 pad_maximum_fusion.2
  526.8 5.6 %copy.23 = f32[4096,256]{1,0:T(8,128)} copy(f32[4096,256]{0,1:T(8,128)} %pad_maximum_fusion.2) | data formatting | bytes 8388608
  (87 shorter events, 11.8 us)
Async XLA Ops:
  7.2 59.4 %all-reduce.6.cloned.1.call-start = ((), (), s32[]{:S(2)}) async-start(), calls=%async_computation | async-start | bytes 524288 | tf_op jit(solution)/shard_map/psum | solution.py:51
  18.1 4.0 copy-start.8
  18.1 208.9 %all-reduce.8.cloned.1.call-start = ((), (), s32[]{:S(2)}) async-start(), calls=%async_computation.1 | async-start | bytes 524288 | tf_op jit(solution)/shard_map/psum | solution.py:51
  66.6 64.2 %copy-start = (f32[256,256]{0,1:T(8,128)S(1)}, f32[256,256]{0,1:T(8,128)}, u32[]{:S(2)}) copy-start(f32[256,256]{0,1:T(8,128)} %all-reduce.6.cloned.1.call-done) | copy-start | bytes 786436
  142.5 49.3 %collective-permute-start = (f32[4096,128]{0,1:T(8,128)S(1)}, f32[4096,128]{0,1:T(8,128)S(1)}, u32[]{:S(2)}, u32[]{:S(2)}) collective-permute-start(f32[4096,128]{0,1:T(8,128)S(1)} %get-tuple-element.69), channel_id=1, source_target_pairs={{0,4},{4,8},{8,12},{12,16},{16,20},{20,24},{24,28},{28,0},{1,5},{5... | collective-permute-start | bytes 6291464 | tf_op jit(solution)/shard_map/ppermute | solution.py:11
  191.8 1.3 copy-start.5
  197.3 186.7 %all-reduce.10.cloned.1.call-start = ((), (), s32[]{:S(2)}) async-start(), calls=%async_computation.2 | async-start | bytes 524288 | tf_op jit(solution)/shard_map/psum | solution.py:51
  227.0 65.1 %copy-start.1 = (f32[256,256]{0,1:T(8,128)S(1)}, f32[256,256]{0,1:T(8,128)}, u32[]{:S(2)}) copy-start(f32[256,256]{0,1:T(8,128)} %all-reduce.8.cloned.1.call-done) | copy-start | bytes 786436
  292.1 2.5 copy-start.6
  299.0 48.9 %collective-permute-start.1 = (f32[4096,128]{0,1:T(8,128)S(1)}, f32[4096,128]{0,1:T(8,128)S(1)}, u32[]{:S(2)}, u32[]{:S(2)}) collective-permute-start(f32[4096,128]{0,1:T(8,128)S(1)} %get-tuple-element.67), channel_id=1, source_target_pairs={{0,4},{4,8},{8,12},{12,16},{16,20},{20,24},{24,28},{28,0},{1,5},{5... | collective-permute-start | bytes 6291464 | tf_op jit(solution)/shard_map/ppermute | solution.py:11
  348.0 1.3 copy-start.3
  384.0 66.9 %copy-start.2 = (f32[256,256]{0,1:T(8,128)S(1)}, f32[256,256]{0,1:T(8,128)}, u32[]{:S(2)}) copy-start(f32[256,256]{0,1:T(8,128)} %all-reduce.10.cloned.1.call-done) | copy-start | bytes 786436
  388.4 0.7 copy-start.7
  450.9 2.5 copy-start.4
  459.2 63.7 %collective-permute-start.2 = (f32[4096,128]{0,1:T(8,128)}, f32[4096,128]{0,1:T(8,128)}, u32[]{:S(2)}, u32[]{:S(2)}) collective-permute-start(f32[4096,128]{0,1:T(8,128)} %get-tuple-element.65), channel_id=1, source_target_pairs={{0,4},{4,8},{8,12},{12,16},{16,20},{20,24},{24,28},{28,0},{1,5},{5... | collective-permute-start | bytes 6291464 | tf_op jit(solution)/shard_map/ppermute | solution.py:11
Sparse Core Ops, SparseCore 0:
  18.2 35.0 all-reduce.5
  197.5 29.4 all-reduce.7
  353.7 30.3 all-reduce.9
where the time goes:
time: 546 us; the launch traced here: 539 us
  other arithmetic  176 us (32%)
  waiting for transfers between devices  153 us (28%)
  blocking collectives  100 us (18%)
  matrix products  51.3 us (9%)
  local copies, waits for them, and re-layouts  29.9 us (5%)
  between operations  23 us (4%)
  starting transfers between devices  5.82 us (1%)
    another operation x20, other arithmetic, make_rotation(): lower = jnp.linalg.cholesky(eye - square)  103 us
    ppermute x3, waiting for transfers between devices, from_behind(): return lax.ppermute(x, axis, [(i, (i + by) % peers) for i in range(peers)])  94.2 us
    another operation x7, other arithmetic, make_rotation(): return jax.scipy.linalg.cho_solve((lower, True), numer)  59.3 us
    psum x3, waiting for transfers between devices, local(): gram = lax.psum(partial_gram, 'rows')  58.7 us
    psum x1, blocking collectives, off_total(): return lax.psum(value, 'pair')  57.4 us
    psum x1, blocking collectives, local(): mean_sq = lax.psum(jnp.sum(matrix * matrix), ('pair', 'rows')) / ncols_all  42.5 us
    dot_general x3, matrix products, local(): lax.dot_general(current, current, (((0,), (0,)), ((), ())), precision=lax...  19.4 us
    dot_general x3, matrix products, local(): turned = jnp.dot(current, rotation, precision=lax.Precision.HIGHEST)  16.8 us
  transfers between devices with their start and end apart: 6, of which 4 were waited for; matrix products, arithmetic and copies ran while one was open for 1% of the time, Pallas kernels for 0%

commit v1 on v0

--- a/solution.py
+++ b/solution.py
@@ -48,7 +48,7 @@
             precision=lax.Precision.HIGHEST,
             preferred_element_type=jnp.float32,
         )
-        gram = lax.psum(partial_gram, "rows")
+        gram = jnp.sum(lax.all_gather(partial_gram, "rows"), axis=0)
         offdiag = gram * (1.0 - eye)
         off_local = jnp.sum(offdiag * offdiag)
         if step == 0:

time: 546 us -> 529 us (0.969)
  waiting for transfers between devices: 153 us -> 123 us
  matrix products: 51.3 us -> 57.2 us
    psum x3 -> x0, waiting for transfers between devices: 58.7 us -> none  [local(): gram = lax.psum(partial_gram, 'rows')]
    all_gather x0 -> x3, waiting for transfers between devices: none -> 26.9 us  [local(): gram = jnp.sum(lax.all_gather(partial_gram, 'rows'), axis=0)]
where the time goes in v1:
time: 529 us; the launch traced here: 521 us
  other arithmetic  180 us (34%)
  waiting for transfers between devices  123 us (23%)
  blocking collectives  101 us (19%)
  matrix products  57.2 us (11%)
  local copies, waits for them, and re-layouts  30.4 us (6%)
  between operations  23.2 us (4%)
  starting transfers between devices  5.43 us (1%)
    another operation x20, other arithmetic, make_rotation(): lower = jnp.linalg.cholesky(eye - square)  103 us
    ppermute x3, waiting for transfers between devices, from_behind(): return lax.ppermute(x, axis, [(i, (i + by) % peers) for i in range(peers)])  96.2 us
    another operation x7, other arithmetic, make_rotation(): return jax.scipy.linalg.cho_solve((lower, True), numer)  59.9 us
    psum x1, blocking collectives, off_total(): return lax.psum(value, 'pair')  59 us
    psum x1, blocking collectives, local(): mean_sq = lax.psum(jnp.sum(matrix * matrix), ('pair', 'rows')) / ncols_all  42.3 us
    all_gather x3, waiting for transfers between devices, local(): gram = jnp.sum(lax.all_gather(partial_gram, 'rows'), axis=0)  26.9 us
    dot_general x3, matrix products, local(): turned = jnp.dot(current, rotation, precision=lax.Precision.HIGHEST)  20.6 us
    dot_general x3, matrix products, local(): lax.dot_general(current, current, (((0,), (0,)), ((), ())), precision=lax...  19.4 us
  transfers between devices with their start and end apart: 6, of which 4 were waited for; matrix products, arithmetic and copies ran while one was open for 1% of the time, Pallas kernels for 0%

profile of v1, /device:TPU:0, one launch (start us, length us, event | category | flops | bytes accessed | tf_op | source)
XLA Modules:
  0.0 521.1 jit_solution(1257010163724016598)
XLA Ops:
  7.2 10.9 %fusion.76 = f32[256,256]{1,0:T(8,128)} fusion(f32[4096,256]{1,0:T(8,128)} %param.5), kind=kOutput, calls=%fused_computation.150 | convolution fusion | flops 3221225472 | bytes 4456448 | tf_op jit(solution)/shard_map/dot_general | solution.py:44
  18.2 3.9 multiply_reduce_fusion
  22.1 42.3 %psum.28 = f32[]{:T(128)} all-reduce(f32[]{:T(128)} %multiply_reduce_fusion), channel_id=1, replica_groups=mesh['pair'=8,'rows'=4] {'pair','rows'}, use_global_device_ids=true, to_apply=%region_2.0 | all-reduce | flops 1 | bytes 8 | tf_op jit(solution)/shard_map/psum | solution.py:40
  66.4 1.3 reduce_sum.63
  67.9 2.8 gather_fusion
  70.7 0.8 fusion.16
  72.2 11.7 %cholesky.172 = f32[128,128]{1,0:T(8,128)S(1)} custom-call(f32[128,128]{1,0:T(8,128)S(1)} %cholesky.270), custom_call_target="Cholesky" | custom-call | tf_op jit(solution)/shard_map/jit(cholesky)/cholesky | solution.py:29
  84.0 9.8 %custom-call.23 = f32[1,128,128]{1,2,0:T(8,128)S(1)} custom-call(f32[1,128,128]{2,1,0:T(8,128)S(1)} %get-tuple-element.85), custom_call_target="InvertDiagBlocksLowerTriangular" | custom-call | tf_op jit(solution)/shard_map/jit(cholesky)/cholesky | solution.py:29
  94.3 11.7 %cholesky.189 = f32[128,128]{1,0:T(8,128)S(1)} custom-call(f32[128,128]{1,0:T(8,128)S(1)} %convolution_subtract_fusion.11), custom_call_target="Cholesky" | custom-call | tf_op jit(solution)/shard_map/jit(cholesky)/cholesky | solution.py:29
  108.1 4.0 while.6
  108.7 1.4 bitcast_dynamic-update-slice_fusion.6
  110.7 1.4 bitcast_dynamic-update-slice_fusion.6
  112.1 19.8 %custom-call.24 = f32[2,128,128]{1,2,0:T(8,128)S(1)} custom-call(f32[2,128,128]{2,1,0:T(8,128)S(1)} %get-tuple-element.24), custom_call_target="InvertDiagBlocksLowerTriangular" | custom-call | tf_op jit(solution)/shard_map/jit(_cho_solve)/triangular_solve | solution.py:30
  133.7 8.8 %convolution_bitcast_fusion = f32[4096,256]{0,1:T(8,128)S(1)} fusion(f32[4096,256]{1,0:T(8,128)} %param.5, f32[128,256]{1,0:T(8,128)S(1)} %fusion.47, f32[128,256]{1,0:T(8,128)S(1)} %fusion.46), kind=kOutput, calls=%fused_computation.9 | convolution fusion | flops 3221291008 | bytes 8650752 | tf_op jit(solution)/shard_map/dot_general | solution.py:61
  142.9 2.3 collective-permute-start
  145.2 47.2 %collective-permute-done = f32[4096,128]{0,1:T(8,128)S(1)} collective-permute-done((f32[4096,128]{0,1:T(8,128)S(1)}, f32[4096,128]{0,1:T(8,128)S(1)}, u32[]{:S(2)}, u32[]{:S(2)}) %collective-permute-start) | collective-permute-done | bytes 2097184 | tf_op jit(solution)/shard_map/ppermute | solution.py:11
  192.4 1.3 copy-done.1
  193.7 4.3 fusion.3
  198.7 13.4 %all-gather.9.cloned.1.call-done = f32[1024,256]{1,0:T(8,128)} async-done(((f32[256,256]{1,0:T(8,128)}), f32[1024,256]{1,0:T(8,128)}) %all-gather.9.cloned.1.call-update) | async-done | bytes 1048592 | tf_op jit(solution)/shard_map/all_gather | solution.py:51
  212.1 1.3 reduce_sum.65
  213.4 2.6 gather_fusion.1
  216.1 1.5 fusion.17
  218.3 11.7 %cholesky.206 = f32[128,128]{1,0:T(8,128)S(1)} custom-call(f32[128,128]{1,0:T(8,128)S(1)} %cholesky.273), custom_call_target="Cholesky" | custom-call | tf_op jit(solution)/shard_map/jit(cholesky)/cholesky | solution.py:29
  230.0 0.7 compare_reduce_fusion.3
  230.7 9.8 %custom-call.25 = f32[1,128,128]{1,2,0:T(8,128)S(1)} custom-call(f32[1,128,128]{2,1,0:T(8,128)S(1)} %get-tuple-element.81), custom_call_target="InvertDiagBlocksLowerTriangular" | custom-call | tf_op jit(solution)/shard_map/jit(cholesky)/cholesky | solution.py:29
  241.1 11.7 %cholesky.223 = f32[128,128]{1,0:T(8,128)S(1)} custom-call(f32[128,128]{1,0:T(8,128)S(1)} %convolution_subtract_fusion.10), custom_call_target="Cholesky" | custom-call | tf_op jit(solution)/shard_map/jit(cholesky)/cholesky | solution.py:29
  252.8 0.7 compare_reduce_fusion.2
  254.9 4.1 while.7
  255.5 1.4 bitcast_dynamic-update-slice_fusion.7
  257.6 1.4 bitcast_dynamic-update-slice_fusion.7
  259.0 20.1 %custom-call.26 = f32[2,128,128]{1,2,0:T(8,128)S(1)} custom-call(f32[2,128,128]{2,1,0:T(8,128)S(1)} %get-tuple-element.25), custom_call_target="InvertDiagBlocksLowerTriangular" | custom-call | tf_op jit(solution)/shard_map/jit(_cho_solve)/triangular_solve | solution.py:30
  279.1 1.2 fusion.33
  280.3 1.2 convolution_subtract_fusion.6
  282.7 5.9 %fusion.2 = f32[4096,256]{0,1:T(8,128)S(1)} fusion(f32[4096,128]{0,1:T(8,128)} %copy-done.1, f32[4096,128]{0,1:T(8,128)S(1)} %get-tuple-element.72, f32[128,256]{1,0:T(8,128)S(1)} %fusion.50, f32[128,256]{1,0:T(8,128)S(1)} %fusion.49), kind=kOutput, calls=%fused_computation.16 | convolution fusion | flops 3222339584 | bytes 8650752 | tf_op jit(solution)/shard_map/dot_general | solution.py:61
  288.9 1.5 collective-permute-start.1
  290.5 49.0 %collective-permute-done.1 = f32[4096,128]{0,1:T(8,128)S(1)} collective-permute-done((f32[4096,128]{0,1:T(8,128)S(1)}, f32[4096,128]{0,1:T(8,128)S(1)}, u32[]{:S(2)}, u32[]{:S(2)}) %collective-permute-start.1) | collective-permute-done | bytes 2097184 | tf_op jit(solution)/shard_map/ppermute | solution.py:11
  339.5 1.3 copy-done
  340.8 4.3 fusion.1
  345.7 13.5 %all-gather.11.cloned.1.call-done = f32[1024,256]{1,0:T(8,128)} async-done(((f32[256,256]{1,0:T(8,128)}), f32[1024,256]{1,0:T(8,128)}) %all-gather.11.cloned.1.call-update) | async-done | bytes 1048592 | tf_op jit(solution)/shard_map/all_gather | solution.py:51
  359.2 1.3 reduce_sum.66
  360.5 2.5 gather_fusion.2
  363.2 1.5 fusion.18
  365.4 0.7 copy-done.2
  366.1 11.7 %cholesky.240 = f32[128,128]{1,0:T(8,128)S(1)} custom-call(f32[128,128]{1,0:T(8,128)S(1)} %cholesky.276), custom_call_target="Cholesky" | custom-call | tf_op jit(solution)/shard_map/jit(cholesky)/cholesky | solution.py:29
  378.5 9.8 %custom-call.27 = f32[1,128,128]{1,2,0:T(8,128)S(1)} custom-call(f32[1,128,128]{2,1,0:T(8,128)S(1)} %get-tuple-element.77), custom_call_target="InvertDiagBlocksLowerTriangular" | custom-call | tf_op jit(solution)/shard_map/jit(cholesky)/cholesky | solution.py:29
  388.3 1.0 constant_dynamic-update-slice_fusion
  389.4 1.1 convolution_subtract_fusion.9
  390.5 11.7 %cholesky.257 = f32[128,128]{1,0:T(8,128)S(1)} custom-call(f32[128,128]{1,0:T(8,128)S(1)} %convolution_subtract_fusion.9), custom_call_target="Cholesky" | custom-call | tf_op jit(solution)/shard_map/jit(cholesky)/cholesky | solution.py:29
  402.2 0.7 compare_reduce_fusion
  404.2 4.0 while.8
  404.8 1.4 bitcast_dynamic-update-slice_fusion.8
  406.8 1.4 bitcast_dynamic-update-slice_fusion.8
  408.2 19.9 %custom-call.28 = f32[2,128,128]{1,2,0:T(8,128)S(1)} custom-call(f32[2,128,128]{2,1,0:T(8,128)S(1)} %get-tuple-element.26), custom_call_target="InvertDiagBlocksLowerTriangular" | custom-call | tf_op jit(solution)/shard_map/jit(_cho_solve)/triangular_solve | solution.py:30
  428.1 1.2 fusion.31
  429.3 1.2 convolution_subtract_fusion.4
  431.7 5.9 %fusion = f32[4096,256]{0,1:T(8,128)S(1)} fusion(f32[4096,128]{0,1:T(8,128)} %copy-done, f32[4096,128]{0,1:T(8,128)S(1)} %get-tuple-element.70, f32[128,256]{1,0:T(8,128)S(1)} %fusion.53, f32[128,256]{1,0:T(8,128)S(1)} %fusion.52), kind=kOutput, calls=%fused_computation.14 | convolution fusion | flops 3222339584 | bytes 8650752 | tf_op jit(solution)/shard_map/dot_general | solution.py:61
  437.6 1.7 slice_select_fusion.1
  439.3 1.5 collective-permute-start.2
  440.7 0.8 fusion.8
  441.5 0.7 fusion.10
  442.2 0.7 fusion.12
  442.8 59.0 %all-reduce.1 = (f32[]{:T(128)}, f32[]{:T(128)}, f32[]{:T(128)}) all-reduce(f32[]{:T(128)} %fusion.12, f32[]{:T(128)} %fusion.10, f32[]{:T(128)} %fusion.8), channel_id=1, replica_groups=mesh['pair'=8,'rows'=4] {'pair'}, use_global_device_ids=true, to_apply=%region_14.17 | all-reduce | flops 3 | bytes 24 | tf_op jit(solution)/shard_map/psum | solution.py:15
  504.6 4.2 pad_maximum_fusion.2
  508.8 5.6 %copy.46 = f32[4096,256]{1,0:T(8,128)} copy(f32[4096,256]{0,1:T(8,128)} %pad_maximum_fusion.2) | data formatting | bytes 8388608
  (83 shorter events, 15.0 us)
Async XLA Ops:
  7.2 59.2 %all-gather.7.cloned.1.call-start = ((), (), s32[]{:S(2)}) async-start(), calls=%async_computation | async-start | bytes 1310720 | tf_op jit(solution)/shard_map/all_gather | solution.py:51
  18.1 46.9 %copy-start.3 = (s32[3,1]{0,1:T(1,128)S(1)}, s32[3,1]{0,1:T(1,128)}, u32[]{:S(2)}) copy-start(s32[3,1]{0,1:T(1,128)} %param.6) | copy-start | bytes 40
  18.2 193.9 %all-gather.9.cloned.1.call-start = ((), (), s32[]{:S(2)}) async-start(), calls=%async_computation.1 | async-start | bytes 1310720 | tf_op jit(solution)/shard_map/all_gather | solution.py:51
  142.9 49.5 %collective-permute-start = (f32[4096,128]{0,1:T(8,128)S(1)}, f32[4096,128]{0,1:T(8,128)S(1)}, u32[]{:S(2)}, u32[]{:S(2)}) collective-permute-start(f32[4096,128]{0,1:T(8,128)S(1)} %get-tuple-element.73), channel_id=1, source_target_pairs={{0,4},{4,8},{8,12},{12,16},{16,20},{20,24},{24,28},{28,0},{1,5},{5... | collective-permute-start | bytes 6291464 | tf_op jit(solution)/shard_map/ppermute | solution.py:11
  192.4 1.3 copy-start.1
  198.0 161.2 %all-gather.11.cloned.1.call-start = ((), (), s32[]{:S(2)}) async-start(), calls=%async_computation.2 | async-start | bytes 1310720 | tf_op jit(solution)/shard_map/all_gather | solution.py:51
  288.9 50.5 %collective-permute-start.1 = (f32[4096,128]{0,1:T(8,128)S(1)}, f32[4096,128]{0,1:T(8,128)S(1)}, u32[]{:S(2)}, u32[]{:S(2)}) collective-permute-start(f32[4096,128]{0,1:T(8,128)S(1)} %get-tuple-element.71), channel_id=1, source_target_pairs={{0,4},{4,8},{8,12},{12,16},{16,20},{20,24},{24,28},{28,0},{1,5},{5... | collective-permute-start | bytes 6291464 | tf_op jit(solution)/shard_map/ppermute | solution.py:11
  339.5 1.3 copy-start
  365.4 0.7 copy-start.2
  439.3 65.3 %collective-permute-start.2 = (f32[4096,128]{0,1:T(8,128)}, f32[4096,128]{0,1:T(8,128)}, u32[]{:S(2)}, u32[]{:S(2)}) collective-permute-start(f32[4096,128]{0,1:T(8,128)} %get-tuple-element.69), channel_id=1, source_target_pairs={{0,4},{4,8},{8,12},{12,16},{16,20},{20,24},{24,28},{28,0},{1,5},{5... | collective-permute-start | bytes 6291464 | tf_op jit(solution)/shard_map/ppermute | solution.py:11
Sparse Core Ops, SparseCore 0:
  18.3 19.9 all-gather.6
  198.1 13.9 all-gather.8
  345.2 13.9 all-gather.10
